TPU v7x, 128 devices: a whole 4x4x4 slice. The times are simulated.
128 devices in a mesh: dom: 32 (over z, y, core), sub: 4 (over x).
Axes of the slice: x: 4, y: 4, z: 4, core: 2. Of those that a mesh axis runs over, the one named last changes fastest.
Arguments:
- charges: float32 [16384, 256], P(('dom', 'sub')), may hold values from -0.3 to 0.3
- points: float32 [3, 16384, 256], P(None, ('dom', 'sub')), may hold values from -1 to 1
- leaf_basis: float32 [16384, 64, 256], P(('dom', 'sub')), may hold values from -0.375 to 0.375
- child_transfer: float32 [16384, 64, 64], P(('dom', 'sub')), may hold values from -0.75 to 0.75
- parent_transfer: float32 [2048, 64, 64], P(('dom', 'sub')), may hold values from -0.75 to 0.75
- nodes_leaf: float32 [3, 16384, 64], P(None, ('dom', 'sub')), may hold values from -2 to 2
- nodes_mid: float32 [3, 2048, 64], P(None, ('dom', 'sub')), may hold values from -2 to 2
- nodes_top: float32 [3, 256, 64], P(None, ('dom', 'sub')), may hold values from -2 to 2
- near_list: int32 [16384, 6], P(('dom', 'sub')), may hold values from -1 to 16383, as said below
- far_leaf: int32 [16384, 16], P(('dom', 'sub')), may hold values from -1 to 16383, as said below
- far_mid: int32 [2048, 16], P(('dom', 'sub')), may hold values from -1 to 2047, as said below
- far_top: int32 [256, 16], P(('dom', 'sub')), may hold values from -1 to 255, as said below
Outputs:
- potential: float32 [16384, 256], P(('dom', 'sub'))
Inputs may be any that keep to these rules, and one draw needn't show every extreme that they name: `near_list`: -1 marks an empty entry; a row's live entries come first, and its first entry is the leaf itself. Row l names only leaves of the aligned block of 128 leaves that holds l or of the blocks beside it. Some rows have all 6 entries live. `far_leaf`: -1 marks an empty entry; a row's live entries come first. Within each aligned block of 128 rows, the entries, empty ones counted, name clusters of each aligned block of 128 clusters exactly 16 times; in some row blocks all entries are live. `far_mid`: -1 marks an empty entry; a row's live entries come first. Within each aligned block of 16 rows, the entries, empty ones counted, name clusters of each aligned block of 16 clusters exactly 2 times; in some row blocks all entries are live. `far_top`: -1 marks an empty entry; a row's live entries come first; in some aligned blocks of 2 rows all entries are live.
All inputs are finite; a program needn't handle non-finite values.
Results may differ from a plain program's by a relative error of at most 0.0003.
Values sent between devices are 32-bit elements; how exact they have to be, the bound alone decides.
No kernel may reach another device: no remote copies, remote signals or barrier semaphores. Data moves between devices by JAX's collectives and lax.ppermute only.
A program may use at most 64 MiB of HBM per device.

v0:
```python
import jax
import jax.numpy as jnp
from jax import lax
from jax.sharding import PartitionSpec as P

soften = 0.25
group_rows = 32


def with_halo(cells, sides, width):
    for axis, dim in sides:
        count = lax.axis_size(axis)
        ends = count - 1
        head = lax.slice_in_dim(cells, 0, width, axis=dim)
        tail = lax.slice_in_dim(cells, cells.shape[dim] - width, cells.shape[dim], axis=dim)
        cells = jnp.concatenate(
            [
                lax.ppermute(tail, axis, [(i, (i + 1) % count) for i in range(ends)]),
                cells,
                lax.ppermute(head, axis, [((i + 1) % count, i) for i in range(ends)]),
            ],
            axis=dim,
        )
    return cells


def kernel(delta_x, delta_y, delta_z):
    return lax.rsqrt(delta_x * delta_x + delta_y * delta_y + delta_z * delta_z + soften)


def near_field(targets, table, picks_all, validity):
    row_count = targets.shape[1]
    width = targets.shape[2]
    groups = row_count // group_rows
    weights_all = validity.astype(jnp.float32)

    def one_group(group):
        start = group * group_rows
        target = lax.dynamic_slice_in_dim(targets, start, group_rows, 1)
        picks = lax.dynamic_slice_in_dim(picks_all, start, group_rows, 0)
        weights = lax.dynamic_slice_in_dim(weights_all, start, group_rows, 0)

        def one_accumulate(column, running):
            chosen = lax.dynamic_index_in_dim(picks, column, 1, keepdims=False)
            weight = lax.dynamic_index_in_dim(weights, column, 1, keepdims=False)
            nearby = jnp.take(table, chosen, axis=0)
            values = kernel(
                target[0][:, :, None] - nearby[:, None, 0:width],
                target[1][:, :, None] - nearby[:, None, width : 2 * width],
                target[2][:, :, None] - nearby[:, None, 2 * width : 3 * width],
            )
            return (
                running + jnp.sum(values * nearby[:, None, 3 * width :], axis=2) * weight[:, None]
            )

        return lax.fori_loop(
            0, picks.shape[1], one_accumulate, jnp.zeros((group_rows, width), jnp.float32)
        )

    return lax.map(one_group, jnp.arange(groups, dtype=jnp.int32)).reshape(row_count, width)


def couple(own_nodes, remote, validity):
    rank_width = own_nodes.shape[2]

    def couple_accumulate(column, running):
        piece = lax.dynamic_index_in_dim(remote, column, 1, keepdims=False)
        weight = lax.dynamic_index_in_dim(validity, column, 1, keepdims=False)
        values = kernel(
            own_nodes[0][:, :, None] - piece[:, None, rank_width : 2 * rank_width],
            own_nodes[1][:, :, None] - piece[:, None, 2 * rank_width : 3 * rank_width],
            own_nodes[2][:, :, None] - piece[:, None, 3 * rank_width :],
        )
        return running + jnp.sum(values * piece[:, None, 0:rank_width], axis=2) * weight[:, None]

    return lax.fori_loop(
        0,
        remote.shape[1],
        couple_accumulate,
        jnp.zeros((own_nodes.shape[1], rank_width), jnp.float32),
    )


def make_table(moments, nodes):
    joined = jnp.concatenate([moments[:, None, :], jnp.transpose(nodes, (1, 0, 2))], axis=1)
    return joined.reshape(moments.shape[0], -1)


def split_ids(lists, per_shard):
    entries = lists.reshape(-1)
    validity = entries >= 0
    owners = jnp.where(validity, entries // per_shard, 0)
    wanted = jnp.where(validity, entries % per_shard, 0)
    return (owners, wanted, validity)


def fetch(table, owners, wanted, validity, capacity):
    shards = lax.axis_size(("dom", "sub"))
    hit_table = (
        (owners[:, None] == jnp.arange(shards, dtype=jnp.int32)[None, :]) & validity[:, None]
    ).astype(jnp.int32)
    rank_slot = jnp.sum((jnp.cumsum(hit_table, axis=0) - 1) * hit_table, axis=1)
    places = jnp.where(validity, owners * capacity + rank_slot, shards * capacity)
    requests = (
        jnp.zeros((shards * capacity,), jnp.int32)
        .at[places]
        .set(wanted, mode="drop")
        .reshape(shards, capacity)
    )
    replies = jnp.take(
        table,
        lax.all_to_all(requests, ("dom", "sub"), split_axis=0, concat_axis=0, tiled=True),
        axis=0,
    )
    answers = lax.all_to_all(replies, ("dom", "sub"), split_axis=0, concat_axis=0, tiled=True)
    flattened = answers.reshape(shards * capacity, table.shape[1])
    return jnp.take(flattened, jnp.minimum(places, shards * capacity - 1), axis=0)


def local(
    charges,
    points,
    leaf_basis,
    child_transfer,
    parent_transfer,
    nodes_leaf,
    nodes_mid,
    nodes_top,
    near_list,
    far_leaf,
    far_mid,
    far_top,
):
    highest = lax.Precision.HIGHEST
    shards = lax.axis_size(("dom", "sub"))
    leaf_count = charges.shape[0]
    mid_count = leaf_count // 8
    top_count = mid_count // 8
    rank_width = leaf_basis.shape[1]
    fan_out = far_leaf.shape[1]
    leaf_moments = jnp.einsum("lrp,lp->lr", leaf_basis, charges, precision=highest)
    mid_moments = (
        jnp.einsum("lij,lj->li", child_transfer, leaf_moments, precision=highest)
        .reshape(mid_count, 8, rank_width)
        .sum(axis=1)
    )
    top_moments = (
        jnp.einsum("lij,lj->li", parent_transfer, mid_moments, precision=highest)
        .reshape(top_count, 8, rank_width)
        .sum(axis=1)
    )
    leaf_table = make_table(leaf_moments, nodes_leaf)
    mid_table = make_table(mid_moments, nodes_mid)
    top_table = make_table(top_moments, nodes_top)
    leaf_owner, leaf_wanted, leaf_valid = split_ids(far_leaf, leaf_count)
    mid_owner, mid_wanted, mid_valid = split_ids(far_mid, mid_count)
    cap_leaf = leaf_count * fan_out // shards
    cap_mid = mid_count * fan_out // shards
    leaf_rows = fetch(leaf_table, leaf_owner, leaf_wanted, leaf_valid, cap_leaf)
    mid_rows = fetch(mid_table, mid_owner, mid_wanted, mid_valid, cap_mid)
    every_top = lax.all_gather(top_table, ("dom", "sub"), axis=0, tiled=True)
    top_rows = jnp.take(every_top, jnp.maximum(far_top.reshape(-1), 0), axis=0)
    leaf_local = couple(
        nodes_leaf,
        leaf_rows.reshape(leaf_count, fan_out, 4 * rank_width),
        leaf_valid.reshape(leaf_count, fan_out).astype(jnp.float32),
    )
    mid_local = couple(
        nodes_mid,
        mid_rows.reshape(mid_count, fan_out, 4 * rank_width),
        mid_valid.reshape(mid_count, fan_out).astype(jnp.float32),
    )
    top_local = couple(
        nodes_top,
        top_rows.reshape(top_count, fan_out, 4 * rank_width),
        (far_top >= 0).astype(jnp.float32),
    )
    mid_down = mid_local + jnp.einsum(
        "lji,lj->li", parent_transfer, jnp.repeat(top_local, 8, axis=0), precision=highest
    )
    leaf_down = leaf_local + jnp.einsum(
        "lji,lj->li", child_transfer, jnp.repeat(mid_down, 8, axis=0), precision=highest
    )
    position = lax.axis_index(("dom", "sub"))
    point_width = charges.shape[1]
    source_rows = jnp.concatenate(
        [jnp.transpose(points, (1, 0, 2)), charges[:, None, :]], axis=1
    ).reshape(leaf_count, 4 * point_width)
    widened = with_halo(source_rows, ((("dom", "sub"), 0),), leaf_count)
    near_valid = near_list >= 0
    near_picks = jnp.where(near_valid, near_list - (position - 1) * leaf_count, 0)
    near_sum = near_field(points, widened, near_picks, near_valid)
    return jnp.einsum("lrp,lr->lp", leaf_basis, leaf_down, precision=highest) + near_sum


def solution(mesh):
    placed = (
        P(("dom", "sub"), None),
        P(None, ("dom", "sub"), None),
        P(("dom", "sub"), None, None),
        P(("dom", "sub"), None, None),
        P(("dom", "sub"), None, None),
        P(None, ("dom", "sub"), None),
        P(None, ("dom", "sub"), None),
        P(None, ("dom", "sub"), None),
        P(("dom", "sub"), None),
        P(("dom", "sub"), None),
        P(("dom", "sub"), None),
        P(("dom", "sub"), None),
    )
    return jax.shard_map(
        local, mesh=mesh, in_specs=placed, out_specs=P(("dom", "sub"), None), check_vma=False
    )
```

profile of v0, /device:TPU:1, one launch (start us, length us, event | category | flops | bytes accessed | tf_op | source)
XLA Modules:
  0.0 462.5 jit_solution(5268315734513533812)
XLA Ops:
  1.2 3.9 collective-permute-start
  5.2 3.7 collective-permute-start.1
  10.7 1.4 scatter_custom_fusion.1
  12.9 9.6 %all-to-all-start.2 = ((s32[128,1,2]{2,1,0:T(1,128)}), s32[128,1,2]{2,1,0:T(1,128)S(1)}, u32[]{:S(2)}, u32[]{:S(2)}) async-start(s32[128,1,2]{2,1,0:T(1,128)} %bitcast.24), calls=%async_computation.2 | async-start | bytes 131072 | tf_op jit(solution)/shard_map/all_to_all | solution.py:112
  29.9 10.3 %fusion.10 = f32[128,1,64]{2,1,0:T(1,128)} fusion(f32[128,64,256]{2,1,0:T(8,128)} %param.24, f32[128,256,1]{1,0,2:T(8,128)S(1)} %bitcast.175), kind=kOutput, calls=%fused_computation.73 | convolution fusion | flops 25165824 | bytes 8552448 | tf_op jit(solution)/shard_map/lrp,lp->lr/dot_general | solution.py:141
  42.4 1.5 fusion.23
  44.0 1.7 multiply_reduce_fusion.5
  49.7 61.8 %all-gather = f32[128,2,256]{2,1,0:T(2,128)S(1)} all-gather(f32[1,2,256]{2,1,0:T(2,128)S(1)} %reshape.658), channel_id=1, replica_groups=mesh['dom'=32,'sub'=4] {'dom','sub'}, dimensions={0}, use_global_device_ids=true | all-gather | bytes 264192 | tf_op jit(solution)/shard_map/all_gather | solution.py:161
  114.6 6.2 %while.70 = (s32[]{:T(128)}, f32[2,64]{1,0:T(2,128)S(1)}, f32[3,2,64]{2,1,0:T(2,128)S(1)}, f32[2,16,256]{2,0,1:T(2,128)S(1)}, f32[2,16]{0,1:T(8,128)S(1)}, /*index=5*/s32[]{:T(128)}, s32[]{:T(128)}) while((s32[]{:T(128)}, f32[2,64]{1,0:T(2,128)S(1)}, f32[3,2,64]{2,1,0:T(2,128)S(1)}, f32[2,16,256]{2,0,1:T(2,128)S(1)}, ...), condition=%wide.region_18.19_spmd.clone, body=%wide.region_16.18_spmd.clone.sunk | while | flops 90371 | bytes 17015 | solution.py:76
  123.2 8.2 %scatter_custom_fusion = s32[2048]{0:T(1024)S(1)} fusion(s32[2048]{0:T(1024)} %bitcast.188, s32[2048]{0:T(1024)} %get-tuple-element.661, s32[]{:T(128)} %constant.350.clone.1), kind=kCustom, calls=%fused_computation.159 | custom fusion | bytes 8704 | tf_op jit(solution)/shard_map/scatter | solution.py:107
  133.8 6.6 %all-to-all-start = ((s32[128,1,16]{2,1,0:T(1,128)}), s32[128,1,16]{2,1,0:T(1,128)S(1)}, u32[]{:S(2)}, u32[]{:S(2)}) async-start(s32[128,1,16]{2,1,0:T(1,128)} %bitcast.8), calls=%async_computation | async-start | bytes 131072 | tf_op jit(solution)/shard_map/all_to_all | solution.py:112
  142.6 7.5 %all-to-all-done = s32[128,1,16]{2,1,0:T(1,128)S(1)} async-done(((s32[128,1,16]{2,1,0:T(1,128)}), s32[128,1,16]{2,1,0:T(1,128)S(1)}, u32[]{:S(2)}, u32[]{:S(2)}) %all-to-all-start) | async-done | bytes 8224 | tf_op jit(solution)/shard_map/all_to_all | solution.py:112
  150.1 5.1 %all-to-all-start.3 = ((f32[128,2,256]{2,1,0:T(2,128)}), f32[128,2,256]{2,1,0:T(2,128)}, u32[]{:S(2)}, u32[]{:S(2)}) async-start(f32[128,2,256]{2,1,0:T(2,128)} %broadcast_select_fusion.3), calls=%async_computation.3 | async-start | bytes 524288 | tf_op jit(solution)/shard_map/all_to_all | solution.py:115
  155.4 6.6 %gather_fusion.1 = f32[2048,256]{1,0:T(8,128)S(1)} fusion(f32[128,256]{1,0:T(8,128)S(1)} %copy.168, s32[2048]{0:T(1024)S(1)} %broadcast_clamp_fusion.1), kind=kCustom, calls=%fused_computation.1 | custom fusion | bytes 4202496 | tf_op jit(solution)/shard_map/jit(_take)/gather | solution.py:110
  162.0 1.7 broadcast_select_fusion.2
  163.7 2.7 all-to-all-done.3
  166.3 7.7 %all-to-all-start.1 = ((f32[128,16,256]{2,1,0:T(8,128)}), f32[128,16,256]{2,1,0:T(8,128)}, u32[]{:S(2)}, u32[]{:S(2)}) async-start(f32[128,16,256]{2,1,0:T(8,128)} %broadcast_select_fusion.2), calls=%async_computation.1 | async-start | bytes 4194304 | tf_op jit(solution)/shard_map/all_to_all | solution.py:115
  175.2 1.9 gather_fusion.4
  178.2 54.2 %while.69 = (s32[]{:T(128)}, f32[16,64]{1,0:T(8,128)S(1)}, f32[3,16,64]{2,1,0:T(8,128)}, f32[16,16,256]{2,0,1:T(8,128)S(1)}, f32[16,16]{0,1:T(8,128)}, /*index=5*/s32[]{:T(128)}, s32[]{:T(128)}) while((s32[]{:T(128)}, f32[16,64]{1,0:T(8,128)S(1)}, f32[3,16,64]{2,1,0:T(8,128)}, f32[16,16,256]{2,0,1:T(8,128)S(1)}, ...), condition=%wide.region_14.15_spmd.clone, body=%wide.region_12.14_spmd.clone.sunk | while | flops 722947 | bytes 135455 | solution.py:76
  233.5 1.3 pad_maximum_fusion
  234.9 157.7 %while.67 = (s32[]{:T(128)}, f32[4,32,256]{2,1,0:T(8,128)S(1)}, s32[4]{0:T(128)S(1)}, s32[128,6]{0,1:T(8,128)S(1)}, f32[128,6]{0,1:T(8,128)S(1)}, /*index=5*/f32...) while((s32[]{:T(128)}, f32[4,32,256]{2,1,0:T(8,128)S(1)}, ...), condition=%wide.region_23.24_spmd, body=%wide.region_19.23_spmd.sunk | while | flops 23119044 | bytes 1614134 | solution.py:60
  237.2 37.1 %while.71 = (s32[]{:T(128)}, f32[32,256]{1,0:T(8,128)S(1)}, f32[3,32,256]{2,1,0:T(8,128)S(1)}, s32[32,6]{0,1:T(8,128)S(1)}, f32[384,1024]{1,0:T(8,128)S(1)}, /*index=5*/f32[32,6]{0,1:T(8,128)S(1)}, s32[]{:T(128)}, s32[]{:T(128)}) while((s32[]{:T(128)}, f32[32,256]{1,0:T(8,128)S(1)}, f32[3,32,256]{2,1,0:T(8,128)S(1)}, ...), condition=%wide.region_22.22_spmd.clone, body=%wide.region_20.21_spmd.clone.sunk | while | flops 23119040 | bytes 1348647 | solution.py:56
  237.9 5.3 %multiply_reduce_fusion.13 = f32[32,256]{1,0:T(8,128)S(1)} fusion(f32[32,256]{1,0:T(8,128)S(1)} %get-tuple-element.908, f32[32,256]{1,0:T(8,128)S(1)} %get-tuple-element.909, f32[32,256]{1,0:T(8,128)S(1)} %get-tuple-element.910, f32[32,256]{1,0:T(8,128)S(1)} %get-tuple-element.911, f32[32,256]{1,0:T(8,128)S(1)} %get-tuple-element.912, ...), kind=kLoop, calls=%fused_computation.8.clone.1 | loop fusion | flops 23060480 | bytes 262144 | tf_op jit(solution)/shard_map/while/body/eval_jaxpr/while/body/eval_jaxpr/reduce_sum | solution.py:53
  244.1 5.3 %multiply_reduce_fusion.13 = f32[32,256]{1,0:T(8,128)S(1)} fusion(f32[32,256]{1,0:T(8,128)S(1)} %get-tuple-element.908, f32[32,256]{1,0:T(8,128)S(1)} %get-tuple-element.909, f32[32,256]{1,0:T(8,128)S(1)} %get-tuple-element.910, f32[32,256]{1,0:T(8,128)S(1)} %get-tuple-element.911, f32[32,256]{1,0:T(8,128)S(1)} %get-tuple-element.912, ...), kind=kLoop, calls=%fused_computation.8.clone.1 | loop fusion | flops 23060480 | bytes 262144 | tf_op jit(solution)/shard_map/while/body/eval_jaxpr/while/body/eval_jaxpr/reduce_sum | solution.py:53
  250.3 5.3 %multiply_reduce_fusion.13 = f32[32,256]{1,0:T(8,128)S(1)} fusion(f32[32,256]{1,0:T(8,128)S(1)} %get-tuple-element.908, f32[32,256]{1,0:T(8,128)S(1)} %get-tuple-element.909, f32[32,256]{1,0:T(8,128)S(1)} %get-tuple-element.910, f32[32,256]{1,0:T(8,128)S(1)} %get-tuple-element.911, f32[32,256]{1,0:T(8,128)S(1)} %get-tuple-element.912, ...), kind=kLoop, calls=%fused_computation.8.clone.1 | loop fusion | flops 23060480 | bytes 262144 | tf_op jit(solution)/shard_map/while/body/eval_jaxpr/while/body/eval_jaxpr/reduce_sum | solution.py:53
  256.5 5.3 %multiply_reduce_fusion.13 = f32[32,256]{1,0:T(8,128)S(1)} fusion(f32[32,256]{1,0:T(8,128)S(1)} %get-tuple-element.908, f32[32,256]{1,0:T(8,128)S(1)} %get-tuple-element.909, f32[32,256]{1,0:T(8,128)S(1)} %get-tuple-element.910, f32[32,256]{1,0:T(8,128)S(1)} %get-tuple-element.911, f32[32,256]{1,0:T(8,128)S(1)} %get-tuple-element.912, ...), kind=kLoop, calls=%fused_computation.8.clone.1 | loop fusion | flops 23060480 | bytes 262144 | tf_op jit(solution)/shard_map/while/body/eval_jaxpr/while/body/eval_jaxpr/reduce_sum | solution.py:53
  262.7 5.3 %multiply_reduce_fusion.13 = f32[32,256]{1,0:T(8,128)S(1)} fusion(f32[32,256]{1,0:T(8,128)S(1)} %get-tuple-element.908, f32[32,256]{1,0:T(8,128)S(1)} %get-tuple-element.909, f32[32,256]{1,0:T(8,128)S(1)} %get-tuple-element.910, f32[32,256]{1,0:T(8,128)S(1)} %get-tuple-element.911, f32[32,256]{1,0:T(8,128)S(1)} %get-tuple-element.912, ...), kind=kLoop, calls=%fused_computation.8.clone.1 | loop fusion | flops 23060480 | bytes 262144 | tf_op jit(solution)/shard_map/while/body/eval_jaxpr/while/body/eval_jaxpr/reduce_sum | solution.py:53
  268.9 5.3 %multiply_reduce_fusion.13 = f32[32,256]{1,0:T(8,128)S(1)} fusion(f32[32,256]{1,0:T(8,128)S(1)} %get-tuple-element.908, f32[32,256]{1,0:T(8,128)S(1)} %get-tuple-element.909, f32[32,256]{1,0:T(8,128)S(1)} %get-tuple-element.910, f32[32,256]{1,0:T(8,128)S(1)} %get-tuple-element.911, f32[32,256]{1,0:T(8,128)S(1)} %get-tuple-element.912, ...), kind=kLoop, calls=%fused_computation.8.clone.1 | loop fusion | flops 23060480 | bytes 262144 | tf_op jit(solution)/shard_map/while/body/eval_jaxpr/while/body/eval_jaxpr/reduce_sum | solution.py:53
  276.6 37.1 %while.71 = (s32[]{:T(128)}, f32[32,256]{1,0:T(8,128)S(1)}, f32[3,32,256]{2,1,0:T(8,128)S(1)}, s32[32,6]{0,1:T(8,128)S(1)}, f32[384,1024]{1,0:T(8,128)S(1)}, /*index=5*/f32[32,6]{0,1:T(8,128)S(1)}, s32[]{:T(128)}, s32[]{:T(128)}) while((s32[]{:T(128)}, f32[32,256]{1,0:T(8,128)S(1)}, f32[3,32,256]{2,1,0:T(8,128)S(1)}, ...), condition=%wide.region_22.22_spmd.clone, body=%wide.region_20.21_spmd.clone.sunk | while | flops 23119040 | bytes 1348647 | solution.py:56
  277.4 5.3 %multiply_reduce_fusion.13 = f32[32,256]{1,0:T(8,128)S(1)} fusion(f32[32,256]{1,0:T(8,128)S(1)} %get-tuple-element.908, f32[32,256]{1,0:T(8,128)S(1)} %get-tuple-element.909, f32[32,256]{1,0:T(8,128)S(1)} %get-tuple-element.910, f32[32,256]{1,0:T(8,128)S(1)} %get-tuple-element.911, f32[32,256]{1,0:T(8,128)S(1)} %get-tuple-element.912, ...), kind=kLoop, calls=%fused_computation.8.clone.1 | loop fusion | flops 23060480 | bytes 262144 | tf_op jit(solution)/shard_map/while/body/eval_jaxpr/while/body/eval_jaxpr/reduce_sum | solution.py:53
  283.6 5.3 %multiply_reduce_fusion.13 = f32[32,256]{1,0:T(8,128)S(1)} fusion(f32[32,256]{1,0:T(8,128)S(1)} %get-tuple-element.908, f32[32,256]{1,0:T(8,128)S(1)} %get-tuple-element.909, f32[32,256]{1,0:T(8,128)S(1)} %get-tuple-element.910, f32[32,256]{1,0:T(8,128)S(1)} %get-tuple-element.911, f32[32,256]{1,0:T(8,128)S(1)} %get-tuple-element.912, ...), kind=kLoop, calls=%fused_computation.8.clone.1 | loop fusion | flops 23060480 | bytes 262144 | tf_op jit(solution)/shard_map/while/body/eval_jaxpr/while/body/eval_jaxpr/reduce_sum | solution.py:53
  289.7 5.3 %multiply_reduce_fusion.13 = f32[32,256]{1,0:T(8,128)S(1)} fusion(f32[32,256]{1,0:T(8,128)S(1)} %get-tuple-element.908, f32[32,256]{1,0:T(8,128)S(1)} %get-tuple-element.909, f32[32,256]{1,0:T(8,128)S(1)} %get-tuple-element.910, f32[32,256]{1,0:T(8,128)S(1)} %get-tuple-element.911, f32[32,256]{1,0:T(8,128)S(1)} %get-tuple-element.912, ...), kind=kLoop, calls=%fused_computation.8.clone.1 | loop fusion | flops 23060480 | bytes 262144 | tf_op jit(solution)/shard_map/while/body/eval_jaxpr/while/body/eval_jaxpr/reduce_sum | solution.py:53
  295.9 5.3 %multiply_reduce_fusion.13 = f32[32,256]{1,0:T(8,128)S(1)} fusion(f32[32,256]{1,0:T(8,128)S(1)} %get-tuple-element.908, f32[32,256]{1,0:T(8,128)S(1)} %get-tuple-element.909, f32[32,256]{1,0:T(8,128)S(1)} %get-tuple-element.910, f32[32,256]{1,0:T(8,128)S(1)} %get-tuple-element.911, f32[32,256]{1,0:T(8,128)S(1)} %get-tuple-element.912, ...), kind=kLoop, calls=%fused_computation.8.clone.1 | loop fusion | flops 23060480 | bytes 262144 | tf_op jit(solution)/shard_map/while/body/eval_jaxpr/while/body/eval_jaxpr/reduce_sum | solution.py:53
  302.1 5.3 %multiply_reduce_fusion.13 = f32[32,256]{1,0:T(8,128)S(1)} fusion(f32[32,256]{1,0:T(8,128)S(1)} %get-tuple-element.908, f32[32,256]{1,0:T(8,128)S(1)} %get-tuple-element.909, f32[32,256]{1,0:T(8,128)S(1)} %get-tuple-element.910, f32[32,256]{1,0:T(8,128)S(1)} %get-tuple-element.911, f32[32,256]{1,0:T(8,128)S(1)} %get-tuple-element.912, ...), kind=kLoop, calls=%fused_computation.8.clone.1 | loop fusion | flops 23060480 | bytes 262144 | tf_op jit(solution)/shard_map/while/body/eval_jaxpr/while/body/eval_jaxpr/reduce_sum | solution.py:53
  308.3 5.3 %multiply_reduce_fusion.13 = f32[32,256]{1,0:T(8,128)S(1)} fusion(f32[32,256]{1,0:T(8,128)S(1)} %get-tuple-element.908, f32[32,256]{1,0:T(8,128)S(1)} %get-tuple-element.909, f32[32,256]{1,0:T(8,128)S(1)} %get-tuple-element.910, f32[32,256]{1,0:T(8,128)S(1)} %get-tuple-element.911, f32[32,256]{1,0:T(8,128)S(1)} %get-tuple-element.912, ...), kind=kLoop, calls=%fused_computation.8.clone.1 | loop fusion | flops 23060480 | bytes 262144 | tf_op jit(solution)/shard_map/while/body/eval_jaxpr/while/body/eval_jaxpr/reduce_sum | solution.py:53
  316.0 37.1 %while.71 = (s32[]{:T(128)}, f32[32,256]{1,0:T(8,128)S(1)}, f32[3,32,256]{2,1,0:T(8,128)S(1)}, s32[32,6]{0,1:T(8,128)S(1)}, f32[384,1024]{1,0:T(8,128)S(1)}, /*index=5*/f32[32,6]{0,1:T(8,128)S(1)}, s32[]{:T(128)}, s32[]{:T(128)}) while((s32[]{:T(128)}, f32[32,256]{1,0:T(8,128)S(1)}, f32[3,32,256]{2,1,0:T(8,128)S(1)}, ...), condition=%wide.region_22.22_spmd.clone, body=%wide.region_20.21_spmd.clone.sunk | while | flops 23119040 | bytes 1348647 | solution.py:56
  316.8 5.3 %multiply_reduce_fusion.13 = f32[32,256]{1,0:T(8,128)S(1)} fusion(f32[32,256]{1,0:T(8,128)S(1)} %get-tuple-element.908, f32[32,256]{1,0:T(8,128)S(1)} %get-tuple-element.909, f32[32,256]{1,0:T(8,128)S(1)} %get-tuple-element.910, f32[32,256]{1,0:T(8,128)S(1)} %get-tuple-element.911, f32[32,256]{1,0:T(8,128)S(1)} %get-tuple-element.912, ...), kind=kLoop, calls=%fused_computation.8.clone.1 | loop fusion | flops 23060480 | bytes 262144 | tf_op jit(solution)/shard_map/while/body/eval_jaxpr/while/body/eval_jaxpr/reduce_sum | solution.py:53
  323.0 5.3 %multiply_reduce_fusion.13 = f32[32,256]{1,0:T(8,128)S(1)} fusion(f32[32,256]{1,0:T(8,128)S(1)} %get-tuple-element.908, f32[32,256]{1,0:T(8,128)S(1)} %get-tuple-element.909, f32[32,256]{1,0:T(8,128)S(1)} %get-tuple-element.910, f32[32,256]{1,0:T(8,128)S(1)} %get-tuple-element.911, f32[32,256]{1,0:T(8,128)S(1)} %get-tuple-element.912, ...), kind=kLoop, calls=%fused_computation.8.clone.1 | loop fusion | flops 23060480 | bytes 262144 | tf_op jit(solution)/shard_map/while/body/eval_jaxpr/while/body/eval_jaxpr/reduce_sum | solution.py:53
  329.2 5.3 %multiply_reduce_fusion.13 = f32[32,256]{1,0:T(8,128)S(1)} fusion(f32[32,256]{1,0:T(8,128)S(1)} %get-tuple-element.908, f32[32,256]{1,0:T(8,128)S(1)} %get-tuple-element.909, f32[32,256]{1,0:T(8,128)S(1)} %get-tuple-element.910, f32[32,256]{1,0:T(8,128)S(1)} %get-tuple-element.911, f32[32,256]{1,0:T(8,128)S(1)} %get-tuple-element.912, ...), kind=kLoop, calls=%fused_computation.8.clone.1 | loop fusion | flops 23060480 | bytes 262144 | tf_op jit(solution)/shard_map/while/body/eval_jaxpr/while/body/eval_jaxpr/reduce_sum | solution.py:53
  335.3 5.3 %multiply_reduce_fusion.13 = f32[32,256]{1,0:T(8,128)S(1)} fusion(f32[32,256]{1,0:T(8,128)S(1)} %get-tuple-element.908, f32[32,256]{1,0:T(8,128)S(1)} %get-tuple-element.909, f32[32,256]{1,0:T(8,128)S(1)} %get-tuple-element.910, f32[32,256]{1,0:T(8,128)S(1)} %get-tuple-element.911, f32[32,256]{1,0:T(8,128)S(1)} %get-tuple-element.912, ...), kind=kLoop, calls=%fused_computation.8.clone.1 | loop fusion | flops 23060480 | bytes 262144 | tf_op jit(solution)/shard_map/while/body/eval_jaxpr/while/body/eval_jaxpr/reduce_sum | solution.py:53
  341.5 5.3 %multiply_reduce_fusion.13 = f32[32,256]{1,0:T(8,128)S(1)} fusion(f32[32,256]{1,0:T(8,128)S(1)} %get-tuple-element.908, f32[32,256]{1,0:T(8,128)S(1)} %get-tuple-element.909, f32[32,256]{1,0:T(8,128)S(1)} %get-tuple-element.910, f32[32,256]{1,0:T(8,128)S(1)} %get-tuple-element.911, f32[32,256]{1,0:T(8,128)S(1)} %get-tuple-element.912, ...), kind=kLoop, calls=%fused_computation.8.clone.1 | loop fusion | flops 23060480 | bytes 262144 | tf_op jit(solution)/shard_map/while/body/eval_jaxpr/while/body/eval_jaxpr/reduce_sum | solution.py:53
  347.7 5.3 %multiply_reduce_fusion.13 = f32[32,256]{1,0:T(8,128)S(1)} fusion(f32[32,256]{1,0:T(8,128)S(1)} %get-tuple-element.908, f32[32,256]{1,0:T(8,128)S(1)} %get-tuple-element.909, f32[32,256]{1,0:T(8,128)S(1)} %get-tuple-element.910, f32[32,256]{1,0:T(8,128)S(1)} %get-tuple-element.911, f32[32,256]{1,0:T(8,128)S(1)} %get-tuple-element.912, ...), kind=kLoop, calls=%fused_computation.8.clone.1 | loop fusion | flops 23060480 | bytes 262144 | tf_op jit(solution)/shard_map/while/body/eval_jaxpr/while/body/eval_jaxpr/reduce_sum | solution.py:53
  355.5 37.1 %while.71 = (s32[]{:T(128)}, f32[32,256]{1,0:T(8,128)S(1)}, f32[3,32,256]{2,1,0:T(8,128)S(1)}, s32[32,6]{0,1:T(8,128)S(1)}, f32[384,1024]{1,0:T(8,128)S(1)}, /*index=5*/f32[32,6]{0,1:T(8,128)S(1)}, s32[]{:T(128)}, s32[]{:T(128)}) while((s32[]{:T(128)}, f32[32,256]{1,0:T(8,128)S(1)}, f32[3,32,256]{2,1,0:T(8,128)S(1)}, ...), condition=%wide.region_22.22_spmd.clone, body=%wide.region_20.21_spmd.clone.sunk | while | flops 23119040 | bytes 1348647 | solution.py:56
  356.2 5.3 %multiply_reduce_fusion.13 = f32[32,256]{1,0:T(8,128)S(1)} fusion(f32[32,256]{1,0:T(8,128)S(1)} %get-tuple-element.908, f32[32,256]{1,0:T(8,128)S(1)} %get-tuple-element.909, f32[32,256]{1,0:T(8,128)S(1)} %get-tuple-element.910, f32[32,256]{1,0:T(8,128)S(1)} %get-tuple-element.911, f32[32,256]{1,0:T(8,128)S(1)} %get-tuple-element.912, ...), kind=kLoop, calls=%fused_computation.8.clone.1 | loop fusion | flops 23060480 | bytes 262144 | tf_op jit(solution)/shard_map/while/body/eval_jaxpr/while/body/eval_jaxpr/reduce_sum | solution.py:53
  362.4 5.3 %multiply_reduce_fusion.13 = f32[32,256]{1,0:T(8,128)S(1)} fusion(f32[32,256]{1,0:T(8,128)S(1)} %get-tuple-element.908, f32[32,256]{1,0:T(8,128)S(1)} %get-tuple-element.909, f32[32,256]{1,0:T(8,128)S(1)} %get-tuple-element.910, f32[32,256]{1,0:T(8,128)S(1)} %get-tuple-element.911, f32[32,256]{1,0:T(8,128)S(1)} %get-tuple-element.912, ...), kind=kLoop, calls=%fused_computation.8.clone.1 | loop fusion | flops 23060480 | bytes 262144 | tf_op jit(solution)/shard_map/while/body/eval_jaxpr/while/body/eval_jaxpr/reduce_sum | solution.py:53
  368.6 5.3 %multiply_reduce_fusion.13 = f32[32,256]{1,0:T(8,128)S(1)} fusion(f32[32,256]{1,0:T(8,128)S(1)} %get-tuple-element.908, f32[32,256]{1,0:T(8,128)S(1)} %get-tuple-element.909, f32[32,256]{1,0:T(8,128)S(1)} %get-tuple-element.910, f32[32,256]{1,0:T(8,128)S(1)} %get-tuple-element.911, f32[32,256]{1,0:T(8,128)S(1)} %get-tuple-element.912, ...), kind=kLoop, calls=%fused_computation.8.clone.1 | loop fusion | flops 23060480 | bytes 262144 | tf_op jit(solution)/shard_map/while/body/eval_jaxpr/while/body/eval_jaxpr/reduce_sum | solution.py:53
  374.8 5.3 %multiply_reduce_fusion.13 = f32[32,256]{1,0:T(8,128)S(1)} fusion(f32[32,256]{1,0:T(8,128)S(1)} %get-tuple-element.908, f32[32,256]{1,0:T(8,128)S(1)} %get-tuple-element.909, f32[32,256]{1,0:T(8,128)S(1)} %get-tuple-element.910, f32[32,256]{1,0:T(8,128)S(1)} %get-tuple-element.911, f32[32,256]{1,0:T(8,128)S(1)} %get-tuple-element.912, ...), kind=kLoop, calls=%fused_computation.8.clone.1 | loop fusion | flops 23060480 | bytes 262144 | tf_op jit(solution)/shard_map/while/body/eval_jaxpr/while/body/eval_jaxpr/reduce_sum | solution.py:53
  381.0 5.3 %multiply_reduce_fusion.13 = f32[32,256]{1,0:T(8,128)S(1)} fusion(f32[32,256]{1,0:T(8,128)S(1)} %get-tuple-element.908, f32[32,256]{1,0:T(8,128)S(1)} %get-tuple-element.909, f32[32,256]{1,0:T(8,128)S(1)} %get-tuple-element.910, f32[32,256]{1,0:T(8,128)S(1)} %get-tuple-element.911, f32[32,256]{1,0:T(8,128)S(1)} %get-tuple-element.912, ...), kind=kLoop, calls=%fused_computation.8.clone.1 | loop fusion | flops 23060480 | bytes 262144 | tf_op jit(solution)/shard_map/while/body/eval_jaxpr/while/body/eval_jaxpr/reduce_sum | solution.py:53
  387.1 5.3 %multiply_reduce_fusion.13 = f32[32,256]{1,0:T(8,128)S(1)} fusion(f32[32,256]{1,0:T(8,128)S(1)} %get-tuple-element.908, f32[32,256]{1,0:T(8,128)S(1)} %get-tuple-element.909, f32[32,256]{1,0:T(8,128)S(1)} %get-tuple-element.910, f32[32,256]{1,0:T(8,128)S(1)} %get-tuple-element.911, f32[32,256]{1,0:T(8,128)S(1)} %get-tuple-element.912, ...), kind=kLoop, calls=%fused_computation.8.clone.1 | loop fusion | flops 23060480 | bytes 262144 | tf_op jit(solution)/shard_map/while/body/eval_jaxpr/while/body/eval_jaxpr/reduce_sum | solution.py:53
  392.6 8.2 %gather_fusion.2 = f32[2048,256]{1,0:T(8,128)S(1)} fusion(f32[2048,256]{1,0:T(8,128)} %bitcast.16, s32[2048]{0:T(1024)S(1)} %copy-done.14), kind=kCustom, calls=%fused_computation.2 | custom fusion | bytes 4202496 | tf_op jit(solution)/shard_map/jit(_take)/gather | solution.py:117
  400.9 1.7 broadcast_select_fusion.1
  402.5 52.8 %while.68 = (s32[]{:T(128)}, f32[128,64]{0,1:T(8,128)S(1)}, f32[3,128,64]{1,2,0:T(8,128)S(1)}, f32[128,16,256]{2,1,0:T(8,128)}, f32[128,16]{0,1:T(8,128)}, /*index=5*/s32[]{:T(128)}, s32[]{:T(128)}) while((s32[]{:T(128)}, f32[128,64]{0,1:T(8,128)S(1)}, f32[3,128,64]{1,2,0:T(8,128)S(1)}, f32[128,16,256]{2,1,0:T(8,128)}, ...), condition=%wide.region_6.7_spmd.clone, body=%wide.region_4.6_spmd.clone.sunk | while | flops 5783555 | bytes 1345119 | solution.py:76
  405.8 1.3 constant_dynamic-slice_fusion.11
  409.1 1.3 constant_dynamic-slice_fusion.11
  412.4 1.3 constant_dynamic-slice_fusion.11
  415.7 1.3 constant_dynamic-slice_fusion.11
  422.3 1.3 constant_dynamic-slice_fusion.11
  425.6 1.3 constant_dynamic-slice_fusion.11
  438.8 1.3 constant_dynamic-slice_fusion.11
  442.1 1.3 constant_dynamic-slice_fusion.11
  445.4 1.3 constant_dynamic-slice_fusion.11
  448.7 1.3 constant_dynamic-slice_fusion.11
  452.0 1.3 constant_dynamic-slice_fusion.11
  455.4 6.4 %fusion.57 = f32[128,1,256]{2,1,0:T(1,128)S(1)} fusion(f32[128,64,1]{1,2,0:T(1,128)S(1)} %copy.201, f32[128,64,256]{2,1,0:T(8,128)} %param.24), kind=kOutput, calls=%fused_computation.200 | convolution fusion | flops 25165824 | bytes 8552448 | tf_op jit(solution)/shard_map/lrp,lr->lp/dot_general | solution.py:193
  (649 shorter events, 155.1 us)
Async XLA Ops:
  0.0 48.6 %copy-start = (f32[16,64,64]{2,1,0:T(8,128)S(1)}, f32[16,64,64]{2,1,0:T(8,128)}, u32[]{:S(2)}) copy-start(f32[16,64,64]{2,1,0:T(8,128)} %param.26) | copy-start | bytes 786436
  0.0 8.9 %copy-start.11 = (s32[16,16]{1,0:T(8,128)S(1)}, s32[16,16]{1,0:T(8,128)}, u32[]{:S(2)}) copy-start(s32[16,16]{1,0:T(8,128)} %param.32) | copy-start | bytes 3076
  0.0 22.6 %copy-start.16 = (s32[128,16]{0,1:T(8,128)S(1)}, s32[128,16]{0,1:T(8,128)}, u32[]{:S(2)}) copy-start(s32[128,16]{0,1:T(8,128)} %param.31) | copy-start | bytes 24580
  0.0 24.2 %copy-start.17 = (s32[2,16]{1,0:T(2,128)S(1)}, s32[2,16]{1,0:T(2,128)}, u32[]{:S(2)}) copy-start(s32[2,16]{1,0:T(2,128)} %param.33) | copy-start | bytes 388
  1.2 232.2 %collective-permute-start = (f32[128,1024]{1,0:T(8,128)S(1)}, f32[128,1024]{1,0:T(8,128)}, u32[]{:S(2)}, u32[]{:S(2)}) collective-permute-start(f32[128,1024]{1,0:T(8,128)S(1)} %bitcast.163), channel_id=1, source_target_pairs={{0,1},{1,2},{2,3},{3,4},{4,5},{5,6},{6,7},{7,8},{8,9},{9,10},{10,1... | collective-permute-start | bytes 1572872 | tf_op jit(solution)/shard_map/ppermute | solution.py:18
  5.2 228.3 %collective-permute-start.1 = (f32[128,1024]{1,0:T(8,128)S(1)}, f32[128,1024]{1,0:T(8,128)}, u32[]{:S(2)}, u32[]{:S(2)}) collective-permute-start(f32[128,1024]{1,0:T(8,128)S(1)} %bitcast.164), channel_id=1, source_target_pairs={{1,0},{2,1},{3,2},{4,3},{5,4},{6,5},{7,6},{8,7},{9,8},{10,9},{11,1... | collective-permute-start | bytes 1572872 | tf_op jit(solution)/shard_map/ppermute | solution.py:20
  12.9 120.9 %all-to-all-start.2 = ((s32[128,1,2]{2,1,0:T(1,128)}), s32[128,1,2]{2,1,0:T(1,128)S(1)}, u32[]{:S(2)}, u32[]{:S(2)}) async-start(s32[128,1,2]{2,1,0:T(1,128)} %bitcast.24), calls=%async_computation.2 | async-start | bytes 131072 | tf_op jit(solution)/shard_map/all_to_all | solution.py:112
  26.4 3.5 copy-start.5
  29.9 14.1 %copy-start.3 = (f32[3,128,64]{1,2,0:T(8,128)S(1)}, f32[3,128,64]{1,2,0:T(8,128)}, u32[]{:S(2)}) copy-start(f32[3,128,64]{1,2,0:T(8,128)} %param.27) | copy-start | bytes 294916
  29.9 14.1 %copy-start.1 = (f32[128,64,64]{0,2,1:T(8,128)S(1)}, f32[128,64,64]{0,2,1:T(8,128)}, u32[]{:S(2)}) copy-start(f32[128,64,64]{0,2,1:T(8,128)} %param.25) | copy-start | bytes 6291460
  40.2 9.3 %copy-start.12 = (f32[3,2,64]{2,1,0:T(2,128)S(1)}, f32[3,2,64]{2,1,0:T(2,128)}, u32[]{:S(2)}) copy-start(f32[3,2,64]{2,1,0:T(2,128)} %param.29) | copy-start | bytes 4612
  41.1 2.9 copy-start.6
  44.0 79.2 %copy-start.4 = (f32[3,16,64]{2,1,0:T(8,128)S(1)}, f32[3,16,64]{2,1,0:T(8,128)}, u32[]{:S(2)}) copy-start(f32[3,16,64]{2,1,0:T(8,128)} %param.28) | copy-start | bytes 36868
  45.7 76.3 %copy-start.15 = (s32[128,6]{0,1:T(8,128)S(1)}, s32[128,6]{0,1:T(8,128)}, u32[]{:S(2)}) copy-start(s32[128,6]{0,1:T(8,128)} %param.30) | copy-start | bytes 9220
  45.7 86.5 %copy-start.7 = (f32[128,16]{1,0:T(8,128)S(1)}, f32[128,16]{1,0:T(8,128)}, u32[]{:S(2)}) copy-start(f32[128,16]{1,0:T(8,128)} %get-tuple-element.657) | copy-start | bytes 24580
  133.8 16.4 %all-to-all-start = ((s32[128,1,16]{2,1,0:T(1,128)}), s32[128,1,16]{2,1,0:T(1,128)S(1)}, u32[]{:S(2)}, u32[]{:S(2)}) async-start(s32[128,1,16]{2,1,0:T(1,128)} %bitcast.8), calls=%async_computation | async-start | bytes 131072 | tf_op jit(solution)/shard_map/all_to_all | solution.py:112
  150.1 16.2 %all-to-all-start.3 = ((f32[128,2,256]{2,1,0:T(2,128)}), f32[128,2,256]{2,1,0:T(2,128)}, u32[]{:S(2)}, u32[]{:S(2)}) async-start(f32[128,2,256]{2,1,0:T(2,128)} %broadcast_select_fusion.3), calls=%async_computation.3 | async-start | bytes 524288 | tf_op jit(solution)/shard_map/all_to_all | solution.py:115
  166.3 226.2 %all-to-all-start.1 = ((f32[128,16,256]{2,1,0:T(8,128)}), f32[128,16,256]{2,1,0:T(8,128)}, u32[]{:S(2)}, u32[]{:S(2)}) async-start(f32[128,16,256]{2,1,0:T(8,128)} %broadcast_select_fusion.2), calls=%async_computation.1 | async-start | bytes 4194304 | tf_op jit(solution)/shard_map/all_to_all | solution.py:115
  175.2 58.1 %copy-start.2 = (f32[128,64,64]{0,2,1:T(8,128)S(1)}, f32[128,64,64]{0,2,1:T(8,128)}, u32[]{:S(2)}) copy-start(f32[128,64,64]{0,2,1:T(8,128)} %param.25) | copy-start | bytes 6291460
  233.4 1.4 copy-start.8
  233.4 1.4 copy-start.9
  233.4 1.4 copy-start.10
  234.9 157.7 %copy-start.14 = (s32[2048]{0:T(1024)S(1)}, s32[2048]{0:T(1024)}, u32[]{:S(2)}) copy-start(s32[2048]{0:T(1024)} %broadcast_clamp_fusion) | copy-start | bytes 24580
  392.6 8.3 %copy-start.13 = (pred[128,16]{1,0:T(8,128)(4,1)S(1)}, pred[128,16]{1,0:T(8,128)(4,1)}, u32[]{:S(2)}) copy-start(pred[128,16]{1,0:T(8,128)(4,1)} %get-tuple-element.658) | copy-start | bytes 6148
where the time goes:
time: 466 us; the launch traced here: 463 us
  other arithmetic  199 us (43%)
  local copies, waits for them, and re-layouts  130 us (28%)
  blocking collectives  61.8 us (13%)
  starting transfers between devices  36.7 us (8%)
  matrix products  18.8 us (4%)
  waiting for transfers between devices  10.2 us (2%)
  loops' own time  5.1 us (1%)
    reduce_sum x24, other arithmetic, one_accumulate(): jnp.sum(values * nearby[:, None, 3 * width:], axis=2) * weight[:, None]  128 us
    all_gather x1, blocking collectives, local(): every_top = lax.all_gather(top_table, ('dom', 'sub'), axis=0, tiled=True)  61.8 us
    reduce_sum x48, other arithmetic, couple_accumulate(): jnp.sum(values * piece[:, None, 0:rank_width], axis=2) * weight[:, None]  31.9 us
    mul x48, local copies, waits for them, and re-layouts, couple_accumulate(): jnp.sum(values * piece[:, None, 0:rank_width], axis=2) * weight[:, None]  30.5 us
    dynamic_slice x32, local copies, waits for them, and re-layouts, couple_accumulate(): piece = lax.dynamic_index_in_dim(remote, column, 1, keepdims=False)  22.7 us
    all_to_all x2, starting transfers between devices, fetch(): lax.all_to_all(requests, ('dom', 'sub'), split_axis=0, concat_axis=0, til...  16.3 us
    gather x24, local copies, waits for them, and re-layouts, one_accumulate(): nearby = jnp.take(table, chosen, axis=0)  14.8 us
    all_to_all x2, starting transfers between devices, fetch(): lax.all_to_all(replies, ('dom', 'sub'), split_axis=0, concat_axis=0, tile...  12.8 us
  transfers between devices with their start and end apart: 6, of which 2 were waited for; matrix products, arithmetic and copies ran while one was open for 60% of the time, Pallas kernels for 0%

commit v1 on v0

--- a/solution.py
+++ b/solution.py
@@ -5,6 +5,16 @@
 
 soften = 0.25
 group_rows = 32
+
+
+def hubs_end(panel):
+    part_next = jnp.concatenate(
+        lax.all_to_all(
+            jnp.stack([panel] * lax.axis_size(("dom", "sub")), axis=0), ("dom", "sub"), 0, 0
+        ),
+        0,
+    )
+    return part_next
 
 
 def with_halo(cells, sides, width):
@@ -158,7 +168,7 @@
     cap_mid = mid_count * fan_out // shards
     leaf_rows = fetch(leaf_table, leaf_owner, leaf_wanted, leaf_valid, cap_leaf)
     mid_rows = fetch(mid_table, mid_owner, mid_wanted, mid_valid, cap_mid)
-    every_top = lax.all_gather(top_table, ("dom", "sub"), axis=0, tiled=True)
+    every_top = hubs_end(top_table)
     top_rows = jnp.take(every_top, jnp.maximum(far_top.reshape(-1), 0), axis=0)
     leaf_local = couple(
         nodes_leaf,

time: 466 us -> 419 us (0.90)
  blocking collectives: 61.8 us -> 0 us
  starting transfers between devices: 36.7 us -> 47.5 us
    all_gather x1 -> x0, blocking collectives: 61.8 us -> none  [local(): every_top = lax.all_gather(top_table, ('dom', 'sub'), axis=0, tiled=True)]
    all_to_all x0 -> x1, starting transfers between devices: none -> 5.07 us  [hubs_end(): lax.all_to_all(jnp.stack([panel] * lax.axis_size(('dom', 'sub')), axis=0)...]
  transfers between devices with their start and end apart: 6 -> 7, of which waited for: 2 -> 3; matrix products, arithmetic and copies ran while one was open for 60% -> 67% of each run, Pallas kernels for 0% -> 0%
where the time goes in v1:
time: 419 us; the launch traced here: 415 us
  other arithmetic  199 us (47%)
  local copies, waits for them, and re-layouts  131 us (31%)
  starting transfers between devices  47.5 us (11%)
  matrix products  19.1 us (5%)
  waiting for transfers between devices  12.3 us (3%)
  loops' own time  5.1 us (1%)
    reduce_sum x24, other arithmetic, one_accumulate(): jnp.sum(values * nearby[:, None, 3 * width:], axis=2) * weight[:, None]  128 us
    reduce_sum x48, other arithmetic, couple_accumulate(): jnp.sum(values * piece[:, None, 0:rank_width], axis=2) * weight[:, None]  31.9 us
    mul x48, local copies, waits for them, and re-layouts, couple_accumulate(): jnp.sum(values * piece[:, None, 0:rank_width], axis=2) * weight[:, None]  30.4 us
    dynamic_slice x32, local copies, waits for them, and re-layouts, couple_accumulate(): piece = lax.dynamic_index_in_dim(remote, column, 1, keepdims=False)  22.7 us
    all_to_all x2, starting transfers between devices, fetch(): lax.all_to_all(requests, ('dom', 'sub'), split_axis=0, concat_axis=0, til...  19.4 us
    all_to_all x2, starting transfers between devices, fetch(): lax.all_to_all(replies, ('dom', 'sub'), split_axis=0, concat_axis=0, tile...  15.3 us
    gather x24, local copies, waits for them, and re-layouts, one_accumulate(): nearby = jnp.take(table, chosen, axis=0)  14.8 us
    add x48, other arithmetic, couple_accumulate(): running + jnp.sum(values * piece[:, None, 0:rank_width], axis=2) * weight...  12.4 us
  transfers between devices with their start and end apart: 7, of which 3 were waited for; matrix products, arithmetic and copies ran while one was open for 67% of the time, Pallas kernels for 0%

profile of v1, /device:TPU:1, one launch (start us, length us, event | category | flops | bytes accessed | tf_op | source)
XLA Modules:
  0.0 415.1 jit_solution(13737973621628310384)
XLA Ops:
  1.2 3.9 collective-permute-start
  5.2 3.7 collective-permute-start.1
  10.8 1.4 scatter_custom_fusion.1
  12.9 9.6 %all-to-all-start.2 = ((s32[128,1,2]{2,1,0:T(1,128)}), s32[128,1,2]{2,1,0:T(1,128)S(1)}, u32[]{:S(2)}, u32[]{:S(2)}) async-start(s32[128,1,2]{2,1,0:T(1,128)} %bitcast.24), calls=%async_computation.2 | async-start | bytes 131072 | tf_op jit(solution)/shard_map/all_to_all | solution.py:122
  29.9 10.6 %fusion.10 = f32[128,1,64]{2,1,0:T(1,128)S(1)} fusion(f32[128,64,256]{2,1,0:T(8,128)} %param.24, f32[128,256,1]{1,0,2:T(8,128)} %bitcast.175), kind=kOutput, calls=%fused_computation.73 | convolution fusion | flops 25165824 | bytes 8552448 | tf_op jit(solution)/shard_map/lrp,lp->lr/dot_general | solution.py:151
  41.9 1.5 fusion.23
  50.1 8.2 %scatter_custom_fusion = s32[2048]{0:T(1024)S(1)} fusion(s32[2048]{0:T(1024)} %bitcast.188, s32[2048]{0:T(1024)} %get-tuple-element.661, s32[]{:T(128)} %constant.350.clone.1), kind=kCustom, calls=%fused_computation.159 | custom fusion | bytes 8704 | tf_op jit(solution)/shard_map/scatter | solution.py:117
  60.0 1.5 copy.170
  64.5 9.8 %all-to-all-start = ((s32[128,1,16]{2,1,0:T(1,128)}), s32[128,1,16]{2,1,0:T(1,128)S(1)}, u32[]{:S(2)}, u32[]{:S(2)}) async-start(s32[128,1,16]{2,1,0:T(1,128)} %bitcast.8), calls=%async_computation | async-start | bytes 131072 | tf_op jit(solution)/shard_map/all_to_all | solution.py:122
  76.5 7.5 %all-to-all-done = s32[128,1,16]{2,1,0:T(1,128)S(1)} async-done(((s32[128,1,16]{2,1,0:T(1,128)}), s32[128,1,16]{2,1,0:T(1,128)S(1)}, u32[]{:S(2)}, u32[]{:S(2)}) %all-to-all-start) | async-done | bytes 8224 | tf_op jit(solution)/shard_map/all_to_all | solution.py:122
  84.7 5.1 %all-to-all-start.4 = ((f32[128,2,256]{2,1,0:T(2,128)}), f32[128,2,256]{2,1,0:T(2,128)}, u32[]{:S(2)}, u32[]{:S(2)}) async-start(f32[128,2,256]{2,1,0:T(2,128)} %stack.3), calls=%async_computation.4 | async-start | bytes 524288 | tf_op jit(solution)/shard_map/all_to_all | solution.py:12
  89.9 6.6 %gather_fusion.1 = f32[2048,256]{1,0:T(8,128)S(1)} fusion(f32[128,256]{1,0:T(8,128)S(1)} %copy.168, s32[2048]{0:T(1024)S(1)} %broadcast_clamp_fusion.1), kind=kCustom, calls=%fused_computation.1 | custom fusion | bytes 4202496 | tf_op jit(solution)/shard_map/jit(_take)/gather | solution.py:120
  96.6 1.7 broadcast_select_fusion.2
  98.3 2.7 all-to-all-done.4
  100.9 7.2 %all-to-all-start.3 = ((f32[128,2,256]{2,1,0:T(2,128)}), f32[128,2,256]{2,1,0:T(2,128)S(1)}, u32[]{:S(2)}, u32[]{:S(2)}) async-start(f32[128,2,256]{2,1,0:T(2,128)} %broadcast_select_fusion.3), calls=%async_computation.3 | async-start | bytes 524288 | tf_op jit(solution)/shard_map/all_to_all | solution.py:125
  110.0 6.2 %while.70 = (s32[]{:T(128)}, f32[2,64]{1,0:T(2,128)S(1)}, f32[3,2,64]{2,1,0:T(2,128)S(1)}, f32[2,16,256]{2,0,1:T(2,128)S(1)}, f32[2,16]{0,1:T(8,128)S(1)}, /*index=5*/s32[]{:T(128)}, s32[]{:T(128)}) while((s32[]{:T(128)}, f32[2,64]{1,0:T(2,128)S(1)}, f32[3,2,64]{2,1,0:T(2,128)S(1)}, f32[2,16,256]{2,0,1:T(2,128)S(1)}, ...), condition=%wide.region_18.19_spmd.clone, body=%wide.region_16.18_spmd.clone.sunk | while | flops 90371 | bytes 17015 | solution.py:86
  117.4 2.2 all-to-all-done.3
  119.5 8.1 %all-to-all-start.1 = ((f32[128,16,256]{2,1,0:T(8,128)}), f32[128,16,256]{2,1,0:T(8,128)}, u32[]{:S(2)}, u32[]{:S(2)}) async-start(f32[128,16,256]{2,1,0:T(8,128)} %broadcast_select_fusion.2), calls=%async_computation.1 | async-start | bytes 4194304 | tf_op jit(solution)/shard_map/all_to_all | solution.py:125
  127.8 1.9 gather_fusion.4
  130.9 54.1 %while.69 = (s32[]{:T(128)}, f32[16,64]{1,0:T(8,128)S(1)}, f32[3,16,64]{2,1,0:T(8,128)}, f32[16,16,256]{2,0,1:T(8,128)S(1)}, f32[16,16]{0,1:T(8,128)}, /*index=5*/s32[]{:T(128)}, s32[]{:T(128)}) while((s32[]{:T(128)}, f32[16,64]{1,0:T(8,128)S(1)}, f32[3,16,64]{2,1,0:T(8,128)}, f32[16,16,256]{2,0,1:T(8,128)S(1)}, ...), condition=%wide.region_14.15_spmd.clone, body=%wide.region_12.14_spmd.clone.sunk | while | flops 722947 | bytes 135455 | solution.py:86
  186.0 1.3 pad_maximum_fusion
  187.4 157.7 %while.67 = (s32[]{:T(128)}, f32[4,32,256]{2,1,0:T(8,128)S(1)}, s32[4]{0:T(128)S(1)}, s32[128,6]{0,1:T(8,128)S(1)}, f32[128,6]{0,1:T(8,128)S(1)}, /*index=5*/f32...) while((s32[]{:T(128)}, f32[4,32,256]{2,1,0:T(8,128)S(1)}, ...), condition=%wide.region_23.24_spmd, body=%wide.region_19.23_spmd.sunk | while | flops 23119044 | bytes 1614134 | solution.py:70
  189.7 37.1 %while.71 = (s32[]{:T(128)}, f32[32,256]{1,0:T(8,128)S(1)}, f32[3,32,256]{2,1,0:T(8,128)S(1)}, s32[32,6]{0,1:T(8,128)S(1)}, f32[384,1024]{1,0:T(8,128)S(1)}, /*index=5*/f32[32,6]{0,1:T(8,128)S(1)}, s32[]{:T(128)}, s32[]{:T(128)}) while((s32[]{:T(128)}, f32[32,256]{1,0:T(8,128)S(1)}, f32[3,32,256]{2,1,0:T(8,128)S(1)}, ...), condition=%wide.region_22.22_spmd.clone, body=%wide.region_20.21_spmd.clone.sunk | while | flops 23119040 | bytes 1348647 | solution.py:66
  190.5 5.3 %multiply_reduce_fusion.13 = f32[32,256]{1,0:T(8,128)S(1)} fusion(f32[32,256]{1,0:T(8,128)S(1)} %get-tuple-element.908, f32[32,256]{1,0:T(8,128)S(1)} %get-tuple-element.909, f32[32,256]{1,0:T(8,128)S(1)} %get-tuple-element.910, f32[32,256]{1,0:T(8,128)S(1)} %get-tuple-element.911, f32[32,256]{1,0:T(8,128)S(1)} %get-tuple-element.912, ...), kind=kLoop, calls=%fused_computation.8.clone.1 | loop fusion | flops 23060480 | bytes 262144 | tf_op jit(solution)/shard_map/while/body/eval_jaxpr/while/body/eval_jaxpr/reduce_sum | solution.py:63
  196.7 5.3 %multiply_reduce_fusion.13 = f32[32,256]{1,0:T(8,128)S(1)} fusion(f32[32,256]{1,0:T(8,128)S(1)} %get-tuple-element.908, f32[32,256]{1,0:T(8,128)S(1)} %get-tuple-element.909, f32[32,256]{1,0:T(8,128)S(1)} %get-tuple-element.910, f32[32,256]{1,0:T(8,128)S(1)} %get-tuple-element.911, f32[32,256]{1,0:T(8,128)S(1)} %get-tuple-element.912, ...), kind=kLoop, calls=%fused_computation.8.clone.1 | loop fusion | flops 23060480 | bytes 262144 | tf_op jit(solution)/shard_map/while/body/eval_jaxpr/while/body/eval_jaxpr/reduce_sum | solution.py:63
  202.9 5.3 %multiply_reduce_fusion.13 = f32[32,256]{1,0:T(8,128)S(1)} fusion(f32[32,256]{1,0:T(8,128)S(1)} %get-tuple-element.908, f32[32,256]{1,0:T(8,128)S(1)} %get-tuple-element.909, f32[32,256]{1,0:T(8,128)S(1)} %get-tuple-element.910, f32[32,256]{1,0:T(8,128)S(1)} %get-tuple-element.911, f32[32,256]{1,0:T(8,128)S(1)} %get-tuple-element.912, ...), kind=kLoop, calls=%fused_computation.8.clone.1 | loop fusion | flops 23060480 | bytes 262144 | tf_op jit(solution)/shard_map/while/body/eval_jaxpr/while/body/eval_jaxpr/reduce_sum | solution.py:63
  209.0 5.3 %multiply_reduce_fusion.13 = f32[32,256]{1,0:T(8,128)S(1)} fusion(f32[32,256]{1,0:T(8,128)S(1)} %get-tuple-element.908, f32[32,256]{1,0:T(8,128)S(1)} %get-tuple-element.909, f32[32,256]{1,0:T(8,128)S(1)} %get-tuple-element.910, f32[32,256]{1,0:T(8,128)S(1)} %get-tuple-element.911, f32[32,256]{1,0:T(8,128)S(1)} %get-tuple-element.912, ...), kind=kLoop, calls=%fused_computation.8.clone.1 | loop fusion | flops 23060480 | bytes 262144 | tf_op jit(solution)/shard_map/while/body/eval_jaxpr/while/body/eval_jaxpr/reduce_sum | solution.py:63
  215.2 5.3 %multiply_reduce_fusion.13 = f32[32,256]{1,0:T(8,128)S(1)} fusion(f32[32,256]{1,0:T(8,128)S(1)} %get-tuple-element.908, f32[32,256]{1,0:T(8,128)S(1)} %get-tuple-element.909, f32[32,256]{1,0:T(8,128)S(1)} %get-tuple-element.910, f32[32,256]{1,0:T(8,128)S(1)} %get-tuple-element.911, f32[32,256]{1,0:T(8,128)S(1)} %get-tuple-element.912, ...), kind=kLoop, calls=%fused_computation.8.clone.1 | loop fusion | flops 23060480 | bytes 262144 | tf_op jit(solution)/shard_map/while/body/eval_jaxpr/while/body/eval_jaxpr/reduce_sum | solution.py:63
  221.4 5.3 %multiply_reduce_fusion.13 = f32[32,256]{1,0:T(8,128)S(1)} fusion(f32[32,256]{1,0:T(8,128)S(1)} %get-tuple-element.908, f32[32,256]{1,0:T(8,128)S(1)} %get-tuple-element.909, f32[32,256]{1,0:T(8,128)S(1)} %get-tuple-element.910, f32[32,256]{1,0:T(8,128)S(1)} %get-tuple-element.911, f32[32,256]{1,0:T(8,128)S(1)} %get-tuple-element.912, ...), kind=kLoop, calls=%fused_computation.8.clone.1 | loop fusion | flops 23060480 | bytes 262144 | tf_op jit(solution)/shard_map/while/body/eval_jaxpr/while/body/eval_jaxpr/reduce_sum | solution.py:63
  229.2 37.1 %while.71 = (s32[]{:T(128)}, f32[32,256]{1,0:T(8,128)S(1)}, f32[3,32,256]{2,1,0:T(8,128)S(1)}, s32[32,6]{0,1:T(8,128)S(1)}, f32[384,1024]{1,0:T(8,128)S(1)}, /*index=5*/f32[32,6]{0,1:T(8,128)S(1)}, s32[]{:T(128)}, s32[]{:T(128)}) while((s32[]{:T(128)}, f32[32,256]{1,0:T(8,128)S(1)}, f32[3,32,256]{2,1,0:T(8,128)S(1)}, ...), condition=%wide.region_22.22_spmd.clone, body=%wide.region_20.21_spmd.clone.sunk | while | flops 23119040 | bytes 1348647 | solution.py:66
  229.9 5.3 %multiply_reduce_fusion.13 = f32[32,256]{1,0:T(8,128)S(1)} fusion(f32[32,256]{1,0:T(8,128)S(1)} %get-tuple-element.908, f32[32,256]{1,0:T(8,128)S(1)} %get-tuple-element.909, f32[32,256]{1,0:T(8,128)S(1)} %get-tuple-element.910, f32[32,256]{1,0:T(8,128)S(1)} %get-tuple-element.911, f32[32,256]{1,0:T(8,128)S(1)} %get-tuple-element.912, ...), kind=kLoop, calls=%fused_computation.8.clone.1 | loop fusion | flops 23060480 | bytes 262144 | tf_op jit(solution)/shard_map/while/body/eval_jaxpr/while/body/eval_jaxpr/reduce_sum | solution.py:63
  236.1 5.3 %multiply_reduce_fusion.13 = f32[32,256]{1,0:T(8,128)S(1)} fusion(f32[32,256]{1,0:T(8,128)S(1)} %get-tuple-element.908, f32[32,256]{1,0:T(8,128)S(1)} %get-tuple-element.909, f32[32,256]{1,0:T(8,128)S(1)} %get-tuple-element.910, f32[32,256]{1,0:T(8,128)S(1)} %get-tuple-element.911, f32[32,256]{1,0:T(8,128)S(1)} %get-tuple-element.912, ...), kind=kLoop, calls=%fused_computation.8.clone.1 | loop fusion | flops 23060480 | bytes 262144 | tf_op jit(solution)/shard_map/while/body/eval_jaxpr/while/body/eval_jaxpr/reduce_sum | solution.py:63
  242.3 5.3 %multiply_reduce_fusion.13 = f32[32,256]{1,0:T(8,128)S(1)} fusion(f32[32,256]{1,0:T(8,128)S(1)} %get-tuple-element.908, f32[32,256]{1,0:T(8,128)S(1)} %get-tuple-element.909, f32[32,256]{1,0:T(8,128)S(1)} %get-tuple-element.910, f32[32,256]{1,0:T(8,128)S(1)} %get-tuple-element.911, f32[32,256]{1,0:T(8,128)S(1)} %get-tuple-element.912, ...), kind=kLoop, calls=%fused_computation.8.clone.1 | loop fusion | flops 23060480 | bytes 262144 | tf_op jit(solution)/shard_map/while/body/eval_jaxpr/while/body/eval_jaxpr/reduce_sum | solution.py:63
  248.5 5.3 %multiply_reduce_fusion.13 = f32[32,256]{1,0:T(8,128)S(1)} fusion(f32[32,256]{1,0:T(8,128)S(1)} %get-tuple-element.908, f32[32,256]{1,0:T(8,128)S(1)} %get-tuple-element.909, f32[32,256]{1,0:T(8,128)S(1)} %get-tuple-element.910, f32[32,256]{1,0:T(8,128)S(1)} %get-tuple-element.911, f32[32,256]{1,0:T(8,128)S(1)} %get-tuple-element.912, ...), kind=kLoop, calls=%fused_computation.8.clone.1 | loop fusion | flops 23060480 | bytes 262144 | tf_op jit(solution)/shard_map/while/body/eval_jaxpr/while/body/eval_jaxpr/reduce_sum | solution.py:63
  254.7 5.3 %multiply_reduce_fusion.13 = f32[32,256]{1,0:T(8,128)S(1)} fusion(f32[32,256]{1,0:T(8,128)S(1)} %get-tuple-element.908, f32[32,256]{1,0:T(8,128)S(1)} %get-tuple-element.909, f32[32,256]{1,0:T(8,128)S(1)} %get-tuple-element.910, f32[32,256]{1,0:T(8,128)S(1)} %get-tuple-element.911, f32[32,256]{1,0:T(8,128)S(1)} %get-tuple-element.912, ...), kind=kLoop, calls=%fused_computation.8.clone.1 | loop fusion | flops 23060480 | bytes 262144 | tf_op jit(solution)/shard_map/while/body/eval_jaxpr/while/body/eval_jaxpr/reduce_sum | solution.py:63
  260.8 5.3 %multiply_reduce_fusion.13 = f32[32,256]{1,0:T(8,128)S(1)} fusion(f32[32,256]{1,0:T(8,128)S(1)} %get-tuple-element.908, f32[32,256]{1,0:T(8,128)S(1)} %get-tuple-element.909, f32[32,256]{1,0:T(8,128)S(1)} %get-tuple-element.910, f32[32,256]{1,0:T(8,128)S(1)} %get-tuple-element.911, f32[32,256]{1,0:T(8,128)S(1)} %get-tuple-element.912, ...), kind=kLoop, calls=%fused_computation.8.clone.1 | loop fusion | flops 23060480 | bytes 262144 | tf_op jit(solution)/shard_map/while/body/eval_jaxpr/while/body/eval_jaxpr/reduce_sum | solution.py:63
  268.6 37.1 %while.71 = (s32[]{:T(128)}, f32[32,256]{1,0:T(8,128)S(1)}, f32[3,32,256]{2,1,0:T(8,128)S(1)}, s32[32,6]{0,1:T(8,128)S(1)}, f32[384,1024]{1,0:T(8,128)S(1)}, /*index=5*/f32[32,6]{0,1:T(8,128)S(1)}, s32[]{:T(128)}, s32[]{:T(128)}) while((s32[]{:T(128)}, f32[32,256]{1,0:T(8,128)S(1)}, f32[3,32,256]{2,1,0:T(8,128)S(1)}, ...), condition=%wide.region_22.22_spmd.clone, body=%wide.region_20.21_spmd.clone.sunk | while | flops 23119040 | bytes 1348647 | solution.py:66
  269.3 5.3 %multiply_reduce_fusion.13 = f32[32,256]{1,0:T(8,128)S(1)} fusion(f32[32,256]{1,0:T(8,128)S(1)} %get-tuple-element.908, f32[32,256]{1,0:T(8,128)S(1)} %get-tuple-element.909, f32[32,256]{1,0:T(8,128)S(1)} %get-tuple-element.910, f32[32,256]{1,0:T(8,128)S(1)} %get-tuple-element.911, f32[32,256]{1,0:T(8,128)S(1)} %get-tuple-element.912, ...), kind=kLoop, calls=%fused_computation.8.clone.1 | loop fusion | flops 23060480 | bytes 262144 | tf_op jit(solution)/shard_map/while/body/eval_jaxpr/while/body/eval_jaxpr/reduce_sum | solution.py:63
  275.5 5.3 %multiply_reduce_fusion.13 = f32[32,256]{1,0:T(8,128)S(1)} fusion(f32[32,256]{1,0:T(8,128)S(1)} %get-tuple-element.908, f32[32,256]{1,0:T(8,128)S(1)} %get-tuple-element.909, f32[32,256]{1,0:T(8,128)S(1)} %get-tuple-element.910, f32[32,256]{1,0:T(8,128)S(1)} %get-tuple-element.911, f32[32,256]{1,0:T(8,128)S(1)} %get-tuple-element.912, ...), kind=kLoop, calls=%fused_computation.8.clone.1 | loop fusion | flops 23060480 | bytes 262144 | tf_op jit(solution)/shard_map/while/body/eval_jaxpr/while/body/eval_jaxpr/reduce_sum | solution.py:63
  281.7 5.3 %multiply_reduce_fusion.13 = f32[32,256]{1,0:T(8,128)S(1)} fusion(f32[32,256]{1,0:T(8,128)S(1)} %get-tuple-element.908, f32[32,256]{1,0:T(8,128)S(1)} %get-tuple-element.909, f32[32,256]{1,0:T(8,128)S(1)} %get-tuple-element.910, f32[32,256]{1,0:T(8,128)S(1)} %get-tuple-element.911, f32[32,256]{1,0:T(8,128)S(1)} %get-tuple-element.912, ...), kind=kLoop, calls=%fused_computation.8.clone.1 | loop fusion | flops 23060480 | bytes 262144 | tf_op jit(solution)/shard_map/while/body/eval_jaxpr/while/body/eval_jaxpr/reduce_sum | solution.py:63
  287.9 5.3 %multiply_reduce_fusion.13 = f32[32,256]{1,0:T(8,128)S(1)} fusion(f32[32,256]{1,0:T(8,128)S(1)} %get-tuple-element.908, f32[32,256]{1,0:T(8,128)S(1)} %get-tuple-element.909, f32[32,256]{1,0:T(8,128)S(1)} %get-tuple-element.910, f32[32,256]{1,0:T(8,128)S(1)} %get-tuple-element.911, f32[32,256]{1,0:T(8,128)S(1)} %get-tuple-element.912, ...), kind=kLoop, calls=%fused_computation.8.clone.1 | loop fusion | flops 23060480 | bytes 262144 | tf_op jit(solution)/shard_map/while/body/eval_jaxpr/while/body/eval_jaxpr/reduce_sum | solution.py:63
  294.1 5.3 %multiply_reduce_fusion.13 = f32[32,256]{1,0:T(8,128)S(1)} fusion(f32[32,256]{1,0:T(8,128)S(1)} %get-tuple-element.908, f32[32,256]{1,0:T(8,128)S(1)} %get-tuple-element.909, f32[32,256]{1,0:T(8,128)S(1)} %get-tuple-element.910, f32[32,256]{1,0:T(8,128)S(1)} %get-tuple-element.911, f32[32,256]{1,0:T(8,128)S(1)} %get-tuple-element.912, ...), kind=kLoop, calls=%fused_computation.8.clone.1 | loop fusion | flops 23060480 | bytes 262144 | tf_op jit(solution)/shard_map/while/body/eval_jaxpr/while/body/eval_jaxpr/reduce_sum | solution.py:63
  300.3 5.3 %multiply_reduce_fusion.13 = f32[32,256]{1,0:T(8,128)S(1)} fusion(f32[32,256]{1,0:T(8,128)S(1)} %get-tuple-element.908, f32[32,256]{1,0:T(8,128)S(1)} %get-tuple-element.909, f32[32,256]{1,0:T(8,128)S(1)} %get-tuple-element.910, f32[32,256]{1,0:T(8,128)S(1)} %get-tuple-element.911, f32[32,256]{1,0:T(8,128)S(1)} %get-tuple-element.912, ...), kind=kLoop, calls=%fused_computation.8.clone.1 | loop fusion | flops 23060480 | bytes 262144 | tf_op jit(solution)/shard_map/while/body/eval_jaxpr/while/body/eval_jaxpr/reduce_sum | solution.py:63
  308.0 37.1 %while.71 = (s32[]{:T(128)}, f32[32,256]{1,0:T(8,128)S(1)}, f32[3,32,256]{2,1,0:T(8,128)S(1)}, s32[32,6]{0,1:T(8,128)S(1)}, f32[384,1024]{1,0:T(8,128)S(1)}, /*index=5*/f32[32,6]{0,1:T(8,128)S(1)}, s32[]{:T(128)}, s32[]{:T(128)}) while((s32[]{:T(128)}, f32[32,256]{1,0:T(8,128)S(1)}, f32[3,32,256]{2,1,0:T(8,128)S(1)}, ...), condition=%wide.region_22.22_spmd.clone, body=%wide.region_20.21_spmd.clone.sunk | while | flops 23119040 | bytes 1348647 | solution.py:66
  308.8 5.3 %multiply_reduce_fusion.13 = f32[32,256]{1,0:T(8,128)S(1)} fusion(f32[32,256]{1,0:T(8,128)S(1)} %get-tuple-element.908, f32[32,256]{1,0:T(8,128)S(1)} %get-tuple-element.909, f32[32,256]{1,0:T(8,128)S(1)} %get-tuple-element.910, f32[32,256]{1,0:T(8,128)S(1)} %get-tuple-element.911, f32[32,256]{1,0:T(8,128)S(1)} %get-tuple-element.912, ...), kind=kLoop, calls=%fused_computation.8.clone.1 | loop fusion | flops 23060480 | bytes 262144 | tf_op jit(solution)/shard_map/while/body/eval_jaxpr/while/body/eval_jaxpr/reduce_sum | solution.py:63
  315.0 5.3 %multiply_reduce_fusion.13 = f32[32,256]{1,0:T(8,128)S(1)} fusion(f32[32,256]{1,0:T(8,128)S(1)} %get-tuple-element.908, f32[32,256]{1,0:T(8,128)S(1)} %get-tuple-element.909, f32[32,256]{1,0:T(8,128)S(1)} %get-tuple-element.910, f32[32,256]{1,0:T(8,128)S(1)} %get-tuple-element.911, f32[32,256]{1,0:T(8,128)S(1)} %get-tuple-element.912, ...), kind=kLoop, calls=%fused_computation.8.clone.1 | loop fusion | flops 23060480 | bytes 262144 | tf_op jit(solution)/shard_map/while/body/eval_jaxpr/while/body/eval_jaxpr/reduce_sum | solution.py:63
  321.1 5.3 %multiply_reduce_fusion.13 = f32[32,256]{1,0:T(8,128)S(1)} fusion(f32[32,256]{1,0:T(8,128)S(1)} %get-tuple-element.908, f32[32,256]{1,0:T(8,128)S(1)} %get-tuple-element.909, f32[32,256]{1,0:T(8,128)S(1)} %get-tuple-element.910, f32[32,256]{1,0:T(8,128)S(1)} %get-tuple-element.911, f32[32,256]{1,0:T(8,128)S(1)} %get-tuple-element.912, ...), kind=kLoop, calls=%fused_computation.8.clone.1 | loop fusion | flops 23060480 | bytes 262144 | tf_op jit(solution)/shard_map/while/body/eval_jaxpr/while/body/eval_jaxpr/reduce_sum | solution.py:63
  327.3 5.3 %multiply_reduce_fusion.13 = f32[32,256]{1,0:T(8,128)S(1)} fusion(f32[32,256]{1,0:T(8,128)S(1)} %get-tuple-element.908, f32[32,256]{1,0:T(8,128)S(1)} %get-tuple-element.909, f32[32,256]{1,0:T(8,128)S(1)} %get-tuple-element.910, f32[32,256]{1,0:T(8,128)S(1)} %get-tuple-element.911, f32[32,256]{1,0:T(8,128)S(1)} %get-tuple-element.912, ...), kind=kLoop, calls=%fused_computation.8.clone.1 | loop fusion | flops 23060480 | bytes 262144 | tf_op jit(solution)/shard_map/while/body/eval_jaxpr/while/body/eval_jaxpr/reduce_sum | solution.py:63
  333.5 5.3 %multiply_reduce_fusion.13 = f32[32,256]{1,0:T(8,128)S(1)} fusion(f32[32,256]{1,0:T(8,128)S(1)} %get-tuple-element.908, f32[32,256]{1,0:T(8,128)S(1)} %get-tuple-element.909, f32[32,256]{1,0:T(8,128)S(1)} %get-tuple-element.910, f32[32,256]{1,0:T(8,128)S(1)} %get-tuple-element.911, f32[32,256]{1,0:T(8,128)S(1)} %get-tuple-element.912, ...), kind=kLoop, calls=%fused_computation.8.clone.1 | loop fusion | flops 23060480 | bytes 262144 | tf_op jit(solution)/shard_map/while/body/eval_jaxpr/while/body/eval_jaxpr/reduce_sum | solution.py:63
  339.7 5.3 %multiply_reduce_fusion.13 = f32[32,256]{1,0:T(8,128)S(1)} fusion(f32[32,256]{1,0:T(8,128)S(1)} %get-tuple-element.908, f32[32,256]{1,0:T(8,128)S(1)} %get-tuple-element.909, f32[32,256]{1,0:T(8,128)S(1)} %get-tuple-element.910, f32[32,256]{1,0:T(8,128)S(1)} %get-tuple-element.911, f32[32,256]{1,0:T(8,128)S(1)} %get-tuple-element.912, ...), kind=kLoop, calls=%fused_computation.8.clone.1 | loop fusion | flops 23060480 | bytes 262144 | tf_op jit(solution)/shard_map/while/body/eval_jaxpr/while/body/eval_jaxpr/reduce_sum | solution.py:63
  345.2 8.2 %gather_fusion.2 = f32[2048,256]{1,0:T(8,128)S(1)} fusion(f32[2048,256]{1,0:T(8,128)} %bitcast.16, s32[2048]{0:T(1024)S(1)} %copy-done.11), kind=kCustom, calls=%fused_computation.2 | custom fusion | bytes 4202496 | tf_op jit(solution)/shard_map/jit(_take)/gather | solution.py:127
  353.4 1.7 broadcast_select_fusion.1
  355.1 52.8 %while.68 = (s32[]{:T(128)}, f32[128,64]{0,1:T(8,128)S(1)}, f32[3,128,64]{1,2,0:T(8,128)S(1)}, f32[128,16,256]{2,1,0:T(8,128)}, f32[128,16]{0,1:T(8,128)}, /*index=5*/s32[]{:T(128)}, s32[]{:T(128)}) while((s32[]{:T(128)}, f32[128,64]{0,1:T(8,128)S(1)}, f32[3,128,64]{1,2,0:T(8,128)S(1)}, f32[128,16,256]{2,1,0:T(8,128)}, ...), condition=%wide.region_6.7_spmd.clone, body=%wide.region_4.6_spmd.clone.sunk | while | flops 5783555 | bytes 1345119 | solution.py:86
  358.4 1.3 constant_dynamic-slice_fusion.11
  361.7 1.3 constant_dynamic-slice_fusion.11
  365.0 1.3 constant_dynamic-slice_fusion.11
  368.3 1.3 constant_dynamic-slice_fusion.11
  371.6 1.3 constant_dynamic-slice_fusion.11
  374.9 1.3 constant_dynamic-slice_fusion.11
  381.5 1.3 constant_dynamic-slice_fusion.11
  384.8 1.3 constant_dynamic-slice_fusion.11
  401.3 1.3 constant_dynamic-slice_fusion.11
  404.6 1.3 constant_dynamic-slice_fusion.11
  408.0 6.4 %fusion.57 = f32[128,1,256]{2,1,0:T(1,128)S(1)} fusion(f32[128,64,1]{1,2,0:T(1,128)S(1)} %copy.201, f32[128,64,256]{2,1,0:T(8,128)} %param.24), kind=kOutput, calls=%fused_computation.200 | convolution fusion | flops 25165824 | bytes 8552448 | tf_op jit(solution)/shard_map/lrp,lr->lp/dot_general | solution.py:203
  (647 shorter events, 157.8 us)
Async XLA Ops:
  0.0 45.8 %copy-start = (f32[16,64,64]{2,1,0:T(8,128)S(1)}, f32[16,64,64]{2,1,0:T(8,128)}, u32[]{:S(2)}) copy-start(f32[16,64,64]{2,1,0:T(8,128)} %param.26) | copy-start | bytes 786436
  0.0 8.9 %copy-start.8 = (s32[16,16]{1,0:T(8,128)S(1)}, s32[16,16]{1,0:T(8,128)}, u32[]{:S(2)}) copy-start(s32[16,16]{1,0:T(8,128)} %param.32) | copy-start | bytes 3076
  0.0 22.6 %copy-start.14 = (s32[128,16]{0,1:T(8,128)S(1)}, s32[128,16]{0,1:T(8,128)}, u32[]{:S(2)}) copy-start(s32[128,16]{0,1:T(8,128)} %param.31) | copy-start | bytes 24580
  0.0 24.3 %copy-start.15 = (s32[2,16]{1,0:T(2,128)S(1)}, s32[2,16]{1,0:T(2,128)}, u32[]{:S(2)}) copy-start(s32[2,16]{1,0:T(2,128)} %param.33) | copy-start | bytes 388
  1.2 184.8 %collective-permute-start = (f32[128,1024]{1,0:T(8,128)S(1)}, f32[128,1024]{1,0:T(8,128)}, u32[]{:S(2)}, u32[]{:S(2)}) collective-permute-start(f32[128,1024]{1,0:T(8,128)S(1)} %bitcast.163), channel_id=1, source_target_pairs={{0,1},{1,2},{2,3},{3,4},{4,5},{5,6},{6,7},{7,8},{8,9},{9,10},{10,1... | collective-permute-start | bytes 1572872 | tf_op jit(solution)/shard_map/ppermute | solution.py:28
  5.2 180.8 %collective-permute-start.1 = (f32[128,1024]{1,0:T(8,128)S(1)}, f32[128,1024]{1,0:T(8,128)}, u32[]{:S(2)}, u32[]{:S(2)}) collective-permute-start(f32[128,1024]{1,0:T(8,128)S(1)} %bitcast.164), channel_id=1, source_target_pairs={{1,0},{2,1},{3,2},{4,3},{5,4},{6,5},{7,6},{8,7},{9,8},{10,9},{11,1... | collective-permute-start | bytes 1572872 | tf_op jit(solution)/shard_map/ppermute | solution.py:30
  12.9 51.5 %all-to-all-start.2 = ((s32[128,1,2]{2,1,0:T(1,128)}), s32[128,1,2]{2,1,0:T(1,128)S(1)}, u32[]{:S(2)}, u32[]{:S(2)}) async-start(s32[128,1,2]{2,1,0:T(1,128)} %bitcast.24), calls=%async_computation.2 | async-start | bytes 131072 | tf_op jit(solution)/shard_map/all_to_all | solution.py:122
  29.9 13.5 %copy-start.3 = (f32[3,128,64]{1,2,0:T(8,128)S(1)}, f32[3,128,64]{1,2,0:T(8,128)}, u32[]{:S(2)}) copy-start(f32[3,128,64]{1,2,0:T(8,128)} %param.27) | copy-start | bytes 294916
  29.9 14.2 %copy-start.1 = (f32[128,64,64]{0,2,1:T(8,128)S(1)}, f32[128,64,64]{0,2,1:T(8,128)}, u32[]{:S(2)}) copy-start(f32[128,64,64]{0,2,1:T(8,128)} %param.25) | copy-start | bytes 6291460
  40.5 9.6 %copy-start.4 = (f32[3,16,64]{2,1,0:T(8,128)S(1)}, f32[3,16,64]{2,1,0:T(8,128)}, u32[]{:S(2)}) copy-start(f32[3,16,64]{2,1,0:T(8,128)} %param.28) | copy-start | bytes 36868
  40.5 9.6 %copy-start.9 = (f32[3,2,64]{2,1,0:T(2,128)S(1)}, f32[3,2,64]{2,1,0:T(2,128)}, u32[]{:S(2)}) copy-start(f32[3,2,64]{2,1,0:T(2,128)} %param.29) | copy-start | bytes 4612
  43.4 2.4 copy-start.12
  64.5 19.5 %all-to-all-start = ((s32[128,1,16]{2,1,0:T(1,128)}), s32[128,1,16]{2,1,0:T(1,128)S(1)}, u32[]{:S(2)}, u32[]{:S(2)}) async-start(s32[128,1,16]{2,1,0:T(1,128)} %bitcast.8), calls=%async_computation | async-start | bytes 131072 | tf_op jit(solution)/shard_map/all_to_all | solution.py:122
  84.7 16.2 %all-to-all-start.4 = ((f32[128,2,256]{2,1,0:T(2,128)}), f32[128,2,256]{2,1,0:T(2,128)}, u32[]{:S(2)}, u32[]{:S(2)}) async-start(f32[128,2,256]{2,1,0:T(2,128)} %stack.3), calls=%async_computation.4 | async-start | bytes 524288 | tf_op jit(solution)/shard_map/all_to_all | solution.py:12
  100.9 18.6 %all-to-all-start.3 = ((f32[128,2,256]{2,1,0:T(2,128)}), f32[128,2,256]{2,1,0:T(2,128)S(1)}, u32[]{:S(2)}, u32[]{:S(2)}) async-start(f32[128,2,256]{2,1,0:T(2,128)} %broadcast_select_fusion.3), calls=%async_computation.3 | async-start | bytes 524288 | tf_op jit(solution)/shard_map/all_to_all | solution.py:125
  119.5 225.6 %all-to-all-start.1 = ((f32[128,16,256]{2,1,0:T(8,128)}), f32[128,16,256]{2,1,0:T(8,128)}, u32[]{:S(2)}, u32[]{:S(2)}) async-start(f32[128,16,256]{2,1,0:T(8,128)} %broadcast_select_fusion.2), calls=%async_computation.1 | async-start | bytes 4194304 | tf_op jit(solution)/shard_map/all_to_all | solution.py:125
  127.6 2.1 copy-start.13
  127.8 58.0 %copy-start.2 = (f32[128,64,64]{0,2,1:T(8,128)S(1)}, f32[128,64,64]{0,2,1:T(8,128)}, u32[]{:S(2)}) copy-start(f32[128,64,64]{0,2,1:T(8,128)} %param.25) | copy-start | bytes 6291460
  186.0 1.4 copy-start.5
  186.0 1.4 copy-start.6
  186.0 1.4 copy-start.7
  187.4 157.7 %copy-start.11 = (s32[2048]{0:T(1024)S(1)}, s32[2048]{0:T(1024)}, u32[]{:S(2)}) copy-start(s32[2048]{0:T(1024)} %broadcast_clamp_fusion) | copy-start | bytes 24580
  345.1 8.3 %copy-start.10 = (pred[128,16]{1,0:T(8,128)(4,1)S(1)}, pred[128,16]{1,0:T(8,128)(4,1)}, u32[]{:S(2)}) copy-start(pred[128,16]{1,0:T(8,128)(4,1)} %get-tuple-element.658) | copy-start | bytes 6148
